TPU v7x, 256 devices: a whole 4x4x8 slice. The times are simulated.
256 devices in a mesh: seq: 32 (over z, y), dp: 8 (over x, core).
Axes of the slice: x: 4, y: 4, z: 8, core: 2. Of those that a mesh axis runs over, the one named last changes fastest.
Arguments:
- queries: bfloat16 [8, 4096, 4096], P('dp', 'seq'), may hold values from -118 to 118
- keys: bfloat16 [8, 4096, 1024], P('dp', 'seq'), may hold values from -9 to 9
- hidden: bfloat16 [8, 4096, 4096], P('dp', 'seq'), may hold values from -6 to 6
- value_weight: bfloat16 [4096, 1024], P('dp'), may hold values from -0.09375 to 0.09375
- readout: bfloat16 [4096, 256], replicated, may hold values from -1.796875 to 1.796875
- base_logits: float32 [8, 4096, 256], P('dp', 'seq'), may hold values from -12 to 300
- labels: int32 [8, 4096], P('dp', 'seq'), may hold values from 0 to 255
- hessian: float32 [1024, 4096], P('seq', 'dp'), may hold values from 0.05 to 2
Outputs:
- estimate: float32 [1024, 4096], P('seq', 'dp')
- hessian_new: float32 [1024, 4096], P('seq', 'dp')
All inputs are finite; a program needn't handle non-finite values.
Results may differ from a plain program's by a relative error of at most 0.033.
Values may be sent and summed in bfloat16 or wider, within the bound.
A program may use at most 64 MiB of HBM per device.

v0:
```python
import math
import jax
import jax.numpy as jnp
from jax import lax
from jax.sharding import PartitionSpec as P

HD = 128
big_negative = -1e30
beta_two = 0.99


def in_blocks(x, dim, count):
    before, after = (x.shape[:dim], x.shape[dim + 1 :])
    return jnp.moveaxis(x.reshape(*before, count, -1, *after), dim, 0)


def sum_at_owner(x, axis, dim):
    blocks = in_blocks(x, dim, lax.axis_size(axis))
    arrived = lax.all_to_all(blocks, axis, split_axis=0, concat_axis=0, tiled=True)
    return arrived.astype(jnp.float32).sum(axis=0)


def cut_rows(length, count):
    turn = length // count
    if turn >= 8:
        turn -= turn % 8
    return [turn * k for k in range(1, count)]


def in_order(blocks, dim):
    shape = list(blocks.shape[1:])
    shape[dim] *= blocks.shape[0]
    return jnp.moveaxis(blocks, 0, dim).reshape(shape)


def several_exchanges(x, axis, pieces, split_dim, concat_dim):
    blocks = in_blocks(x, split_dim, lax.axis_size(axis))
    cut = max(range(1, max(2, blocks.ndim - 1)), key=lambda d: blocks.shape[d])
    done = []
    for share in jnp.split(blocks, cut_rows(blocks.shape[cut], pieces), axis=cut):
        if share.size:
            done.append(lax.all_to_all(share, axis, split_axis=0, concat_axis=0, tiled=True))
    return in_order(jnp.concatenate(done, axis=cut), concat_dim)


def sent_to_all(x, axis):
    copies = jnp.broadcast_to(x, (lax.axis_size(axis), *x.shape))
    return lax.all_to_all(copies, axis, split_axis=0, concat_axis=0, tiled=True)


def collect(x, axis, dim):
    return in_order(sent_to_all(x, axis), dim)


def block_scores(q_block, k_block, row_start, col_start, scale):
    scores = (
        jnp.einsum("hqd,hkd->hqk", q_block, k_block, preferred_element_type=jnp.float32) * scale
    )
    rows_pos = row_start + lax.broadcasted_iota(jnp.int32, scores.shape, 1)
    cols_pos = col_start + lax.broadcasted_iota(jnp.int32, scores.shape, 2)
    return jnp.where(cols_pos <= rows_pos, scores, big_negative)


def row_statistics(queries, keys, width, scale):
    heads, length, _ = queries.shape
    blocks = length // width

    def row_outer(i, state):
        i = jnp.asarray(i).astype(jnp.int32)
        peak_all, total_all = state
        q_block = lax.dynamic_slice_in_dim(queries, i * width, width, 1)

        def row_inner(j, carry):
            j = jnp.asarray(j).astype(jnp.int32)
            peak, total = carry
            k_block = lax.dynamic_slice_in_dim(keys, j * width, width, 1)
            scores = block_scores(q_block, k_block, i * width, j * width, scale)
            fresh = jnp.maximum(peak, jnp.max(scores, axis=2))
            total = total * jnp.exp(peak - fresh) + jnp.sum(
                jnp.exp(scores - fresh[:, :, None]), axis=2
            )
            return (fresh, total)

        starting = (
            jnp.full((heads, width), big_negative, jnp.float32),
            jnp.zeros((heads, width), jnp.float32),
        )
        peak, total = lax.fori_loop(0, i + 1, row_inner, starting)
        peak_all = lax.dynamic_update_slice_in_dim(peak_all, peak, i * width, 1)
        total_all = lax.dynamic_update_slice_in_dim(total_all, total, i * width, 1)
        return (peak_all, total_all)

    starting = (jnp.zeros((heads, length), jnp.float32), jnp.zeros((heads, length), jnp.float32))
    return lax.fori_loop(0, blocks, row_outer, starting)


def attend(queries, keys, values, peak, total, width, scale):
    heads, length, dim = queries.shape
    blocks = length // width

    def attend_outer(i, output):
        i = jnp.asarray(i).astype(jnp.int32)
        q_block = lax.dynamic_slice_in_dim(queries, i * width, width, 1)
        peak_block = lax.dynamic_slice_in_dim(peak, i * width, width, 1)
        total_block = lax.dynamic_slice_in_dim(total, i * width, width, 1)

        def attend_inner(j, running):
            j = jnp.asarray(j).astype(jnp.int32)
            k_block = lax.dynamic_slice_in_dim(keys, j * width, width, 1)
            v_block = lax.dynamic_slice_in_dim(values, j * width, width, 1)
            scores = block_scores(q_block, k_block, i * width, j * width, scale)
            weights = (jnp.exp(scores - peak_block[:, :, None]) / total_block[:, :, None]).astype(
                jnp.bfloat16
            )
            return running + jnp.einsum(
                "hqk,hkd->hqd", weights, v_block, preferred_element_type=jnp.float32
            )

        running = lax.fori_loop(0, i + 1, attend_inner, jnp.zeros((heads, width, dim), jnp.float32))
        return lax.dynamic_update_slice_in_dim(output, running.astype(jnp.bfloat16), i * width, 1)

    return lax.fori_loop(0, blocks, attend_outer, jnp.zeros((heads, length, dim), jnp.bfloat16))


def value_grads(queries, keys, d_out, peak, total, width, scale):
    heads, length, dim = queries.shape
    blocks = length // width

    def value_outer(j, output):
        j = jnp.asarray(j).astype(jnp.int32)
        k_block = lax.dynamic_slice_in_dim(keys, j * width, width, 1)

        def value_inner(i, running):
            i = jnp.asarray(i).astype(jnp.int32)
            q_block = lax.dynamic_slice_in_dim(queries, i * width, width, 1)
            d_block = lax.dynamic_slice_in_dim(d_out, i * width, width, 1)
            peak_block = lax.dynamic_slice_in_dim(peak, i * width, width, 1)
            total_block = lax.dynamic_slice_in_dim(total, i * width, width, 1)
            scores = block_scores(q_block, k_block, i * width, j * width, scale)
            weights = (jnp.exp(scores - peak_block[:, :, None]) / total_block[:, :, None]).astype(
                jnp.bfloat16
            )
            return running + jnp.einsum(
                "hqk,hqd->hkd", weights, d_block, preferred_element_type=jnp.float32
            )

        running = lax.fori_loop(j, blocks, value_inner, jnp.zeros((heads, width, dim), jnp.float32))
        return lax.dynamic_update_slice_in_dim(output, running.astype(jnp.bfloat16), j * width, 1)

    return lax.fori_loop(0, blocks, value_outer, jnp.zeros((heads, length, dim), jnp.bfloat16))


def local(queries, keys, hidden, value_weight, readout, base_logits, labels, hessian):
    seq_count = lax.axis_size("seq")
    data_count = lax.axis_size("dp")
    token_rows = queries.shape[1]
    heads = queries.shape[2] // HD
    kv_heads = keys.shape[2] // HD
    kv_width = keys.shape[2]
    group = heads // kv_heads
    local_heads = heads // seq_count
    spread_factor = max(1, group // local_heads)
    local_kv = kv_heads * spread_factor // seq_count
    length = token_rows * seq_count
    width = min(512, length)
    scale = 1.0 / math.sqrt(HD)
    columns = lax.all_to_all(hidden, "dp", split_axis=2, concat_axis=0, tiled=True)
    values = sum_at_owner(
        jnp.einsum("std,dk->stk", columns, value_weight, preferred_element_type=jnp.float32).astype(
            jnp.bfloat16
        ),
        "dp",
        0,
    )
    values = values.astype(jnp.bfloat16)

    def widen(array):
        split = array.reshape(1, token_rows, kv_heads, 1, HD)
        split = jnp.broadcast_to(split, (1, token_rows, kv_heads, spread_factor, HD))
        return split.reshape(1, token_rows, seq_count, local_kv * HD)

    paired = jnp.concatenate((widen(keys), widen(values)), axis=3)
    paired = paired.reshape(1, token_rows, seq_count * 2 * local_kv * HD)
    head_queries, head_pairs = (
        several_exchanges(queries, "seq", 2, 2, 1),
        several_exchanges(paired, "seq", 2, 2, 1),
    )

    def heads_first(array, count):
        return array[0].reshape(length, count, HD).transpose(1, 0, 2)

    q_local = heads_first(head_queries, local_heads)
    pair_local = head_pairs[0].reshape(length, 2, local_kv, HD)
    k_local = jnp.repeat(pair_local[:, 0].transpose(1, 0, 2), local_heads // local_kv, axis=0)
    v_local = jnp.repeat(pair_local[:, 1].transpose(1, 0, 2), local_heads // local_kv, axis=0)
    peak, total = row_statistics(q_local, k_local, width, scale)
    attended = attend(q_local, k_local, v_local, peak, total, width, scale)
    attended = attended.transpose(1, 0, 2).reshape(1, length, local_heads * HD)
    mixed = several_exchanges(attended, "seq", 2, 1, 2)
    logits = base_logits[0] + jnp.dot(mixed[0], readout, preferred_element_type=jnp.float32)
    softmax_rows = jax.nn.softmax(logits, axis=1)
    chosen = labels[0][:, None] == lax.broadcasted_iota(jnp.int32, logits.shape, 1)
    d_logits = (softmax_rows - chosen.astype(jnp.float32)).astype(jnp.bfloat16)
    d_mixed = jnp.einsum("tc,ec->te", d_logits, readout, preferred_element_type=jnp.float32).astype(
        jnp.bfloat16
    )
    d_heads = several_exchanges(d_mixed[None], "seq", 2, 2, 1)
    d_local = heads_first(d_heads, local_heads)
    d_head = value_grads(q_local, k_local, d_local, peak, total, width, scale)
    d_head = d_head.transpose(1, 0, 2).reshape(1, length, local_heads * HD)
    d_tokens = lax.all_to_all(d_head, "seq", split_axis=1, concat_axis=2, tiled=True)
    d_values = d_tokens[0].astype(jnp.float32).reshape(token_rows, kv_heads, group, HD).sum(axis=2)
    d_values = d_values.reshape(1, token_rows, kv_width).astype(jnp.bfloat16)
    partial_value = jnp.einsum(
        "stk,std->kd", collect(d_values, "dp", 0), columns, preferred_element_type=jnp.float32
    )
    grad_sum = sum_at_owner(partial_value.astype(jnp.bfloat16), "seq", 0)
    tokens_all = length * data_count
    estimate = grad_sum * grad_sum / tokens_all
    return (estimate, beta_two * hessian + (1.0 - beta_two) * estimate)


def solution(mesh):
    placed = (
        P("dp", "seq", None),
        P("dp", "seq", None),
        P("dp", "seq", None),
        P("dp", None),
        P(),
        P("dp", "seq", None),
        P("dp", "seq"),
        P("seq", "dp"),
    )
    return jax.shard_map(
        local,
        mesh=mesh,
        in_specs=placed,
        out_specs=(P("seq", "dp"), P("seq", "dp")),
        check_vma=False,
    )
```

profile of v0, /device:TPU:8, one launch (start us, length us, event | category | flops | bytes accessed | tf_op | source)
XLA Modules:
  0.0 691.2 jit_solution(15799862219191184211)
XLA Ops:
  0.6 5.7 copy.51
  6.8 23.3 %reduce.11 = bf16[4096,128]{1,0:T(8,128)(2,1)S(1)} reduce(bf16[4096,1,128]{2,1,0:T(2,128)(2,1)} %bitcast.184, bf16[]{:T(256)} %broadcast.149), dimensions={1}, to_apply=%bitcast.130.reduce_sub_computation | reduce | bytes 2097154
  31.3 4.3 all-to-all-start
  39.0 2.4 copy.59
  41.3 10.3 %all-to-all-done = bf16[8,2,32768]{2,1,0:T(2,128)(2,1)} async-done(((bf16[8,2,32768]{2,1,0:T(2,128)(2,1)}), bf16[8,2,32768]{2,1,0:T(2,128)(2,1)}, u32[]{:S(2)}, u32[]{:S(2)}) %all-to-all-start) | async-done | bytes 1048608 | tf_op jit(solution)/shard_map/all_to_all | solution.py:167
  51.6 11.8 %all-to-all-start.4 = ((bf16[32,1,64,128]{3,2,1,0:T(8,128)(2,1)}), bf16[32,1,64,128]{3,2,1,0:T(8,128)(2,1)}, u32[]{:S(2)}, u32[]{:S(2)}) async-start(bf16[32,1,64,128]{3,2,1,0:T(8,128)(2,1)} %copy.59), calls=%async_computation.4 | async-start | bytes 1048576 | tf_op jit(solution)/shard_map/all_to_all | solution.py:42
  63.4 5.8 reshape.162
  72.2 4.1 convert_bitcast_fusion
  76.3 3.6 all-to-all-done.4
  80.0 4.4 all-to-all-start.1
  85.5 26.0 %all-to-all-done.1 = bf16[8,1,128,1024]{3,2,1,0:T(8,128)(2,1)} async-done(((bf16[8,1,128,1024]{3,2,1,0:T(8,128)(2,1)}), bf16[8,1,128,1024]{3,2,1,0:T(8,128)(2,1)}, u32[]{:S(2)}, u32[]{:S(2)}) %all-to-all-start.1) | async-done | bytes 2097184 | tf_op jit(solution)/shard_map/all_to_all | solution.py:19
  111.5 6.3 all-to-all-start.5
  122.1 12.3 %all-to-all-done.5 = bf16[32,1,64,128]{3,2,1,0:T(8,128)(2,1)} async-done(((bf16[32,1,64,128]{3,2,1,0:T(8,128)(2,1)}), bf16[32,1,64,128]{3,2,1,0:T(8,128)(2,1)}, u32[]{:S(2)}, u32[]{:S(2)}) %all-to-all-start.5) | async-done | bytes 524320 | tf_op jit(solution)/shard_map/all_to_all | solution.py:42
  134.4 32.7 %all_to_all.82 = bf16[32,1,64,256]{3,2,1,0:T(8,128)(2,1)} all-to-all(bf16[32,1,64,256]{3,2,1,0:T(8,128)(2,1)S(1)} %get-tuple-element.816), channel_id=1, replica_groups=mesh['seq'=32,'dp'=8] {'seq'}, dimensions={0} | all-to-all | bytes 2097152 | tf_op jit(solution)/shard_map/all_to_all | solution.py:42
  167.1 5.6 all-to-all-start.3
  174.0 25.5 %all-to-all-done.3 = bf16[32,1,64,256]{3,2,1,0:T(8,128)(2,1)} async-done(((bf16[32,1,64,256]{3,2,1,0:T(8,128)(2,1)}), bf16[32,1,64,256]{3,2,1,0:T(8,128)(2,1)}, u32[]{:S(2)}, u32[]{:S(2)}) %all-to-all-start.3) | async-done | bytes 1048608 | tf_op jit(solution)/shard_map/all_to_all | solution.py:42
  199.6 3.1 pad_maximum_fusion
  202.7 4.0 reshape.160
  206.6 6.8 fusion.74
  213.4 5.4 copy.75
  218.9 2.3 copy.69
  222.4 59.3 %while.120 = (s32[]{:T(128)}, f32[1,4096]{1,0:T(1,128)}, f32[1,4096]{1,0:T(1,128)}, bf16[1,4096,128]{2,1,0:T(8,128)(2,1)S(1)}, bf16[1,4096,128]{2,1,0:T(8,128)(2...) while((s32[]{:T(128)}, f32[1,4096]{1,0:T(1,128)}, ...), condition=%wide.region_6.7_spmd, body=%wide.region_1.6_spmd.sunk | while | flops 68683792 | bytes 2669010 | solution.py:94
  224.5 3.0 while.125
  228.2 4.5 while.125
  233.4 6.0 while.125
  240.0 7.5 %while.125 = (s32[]{:T(128)}, f32[1,512]{1,0:T(1,128)S(1)}, f32[1,512]{1,0:T(1,128)S(1)}, s32[]{:T(128)}, s32[]{:T(128)}, /*index=5*/bf16[1,4096,128]{2,1,0:T(8,...) while((s32[]{:T(128)}, f32[1,512]{1,0:T(1,128)S(1)}, ...), condition=%wide.region_5.5_spmd, body=%wide.region_2.4_spmd.sunk | while | flops 68683784 | bytes 2394279 | solution.py:88
  248.2 9.0 %while.125 = (s32[]{:T(128)}, f32[1,512]{1,0:T(1,128)S(1)}, f32[1,512]{1,0:T(1,128)S(1)}, s32[]{:T(128)}, s32[]{:T(128)}, /*index=5*/bf16[1,4096,128]{2,1,0:T(8,...) while((s32[]{:T(128)}, f32[1,512]{1,0:T(1,128)S(1)}, ...), condition=%wide.region_5.5_spmd, body=%wide.region_2.4_spmd.sunk | while | flops 68683784 | bytes 2394279 | solution.py:88
  257.9 10.5 %while.125 = (s32[]{:T(128)}, f32[1,512]{1,0:T(1,128)S(1)}, f32[1,512]{1,0:T(1,128)S(1)}, s32[]{:T(128)}, s32[]{:T(128)}, /*index=5*/bf16[1,4096,128]{2,1,0:T(8,...) while((s32[]{:T(128)}, f32[1,512]{1,0:T(1,128)S(1)}, ...), condition=%wide.region_5.5_spmd, body=%wide.region_2.4_spmd.sunk | while | flops 68683784 | bytes 2394279 | solution.py:88
  269.0 12.1 %while.125 = (s32[]{:T(128)}, f32[1,512]{1,0:T(1,128)S(1)}, f32[1,512]{1,0:T(1,128)S(1)}, s32[]{:T(128)}, s32[]{:T(128)}, /*index=5*/bf16[1,4096,128]{2,1,0:T(8,...) while((s32[]{:T(128)}, f32[1,512]{1,0:T(1,128)S(1)}, ...), condition=%wide.region_5.5_spmd, body=%wide.region_2.4_spmd.sunk | while | flops 68683784 | bytes 2394279 | solution.py:88
  281.7 5.4 copy.76
  287.1 2.3 copy.63
  290.5 74.3 %while.122 = (s32[]{:T(128)}, bf16[1,4096,128]{2,1,0:T(8,128)(2,1)}, bf16[1,4096,128]{2,1,0:T(8,128)(2,1)S(1)}, f32[1,4096]{1,0:T(1,128)}, f32[1,4096]{1,0:T(1,1...) while((s32[]{:T(128)}, bf16[1,4096,128]{2,1,0:T(8,128)(2,1)}, ...), condition=%wide.region_10.11_spmd, body=%wide.region_7.10_spmd.sunk | while | flops 135922688 | bytes 1857014 | solution.py:122
  294.4 3.5 while.126
  299.4 5.2 while.126
  306.0 7.0 %while.126 = (s32[]{:T(128)}, f32[1,512,128]{2,1,0:T(8,128)S(1)}, s32[]{:T(128)}, s32[]{:T(128)}, bf16[1,4096,128]{2,1,0:T(8,128)(2,1)}, /*index=5*/bf16[1,512,1...) while((s32[]{:T(128)}, f32[1,512,128]{2,1,0:T(8,128)S(1)}, ...), condition=%wide.region_9.9_spmd, body=%wide.region_8.8_spmd.sunk | while | flops 135857152 | bytes 930995 | solution.py:119
  314.4 8.7 %while.126 = (s32[]{:T(128)}, f32[1,512,128]{2,1,0:T(8,128)S(1)}, s32[]{:T(128)}, s32[]{:T(128)}, bf16[1,4096,128]{2,1,0:T(8,128)(2,1)}, /*index=5*/bf16[1,512,1...) while((s32[]{:T(128)}, f32[1,512,128]{2,1,0:T(8,128)S(1)}, ...), condition=%wide.region_9.9_spmd, body=%wide.region_8.8_spmd.sunk | while | flops 135857152 | bytes 930995 | solution.py:119
  324.6 10.5 %while.126 = (s32[]{:T(128)}, f32[1,512,128]{2,1,0:T(8,128)S(1)}, s32[]{:T(128)}, s32[]{:T(128)}, bf16[1,4096,128]{2,1,0:T(8,128)(2,1)}, /*index=5*/bf16[1,512,1...) while((s32[]{:T(128)}, f32[1,512,128]{2,1,0:T(8,128)S(1)}, ...), condition=%wide.region_9.9_spmd, body=%wide.region_8.8_spmd.sunk | while | flops 135857152 | bytes 930995 | solution.py:119
  336.5 12.2 %while.126 = (s32[]{:T(128)}, f32[1,512,128]{2,1,0:T(8,128)S(1)}, s32[]{:T(128)}, s32[]{:T(128)}, bf16[1,4096,128]{2,1,0:T(8,128)(2,1)}, /*index=5*/bf16[1,512,1...) while((s32[]{:T(128)}, f32[1,512,128]{2,1,0:T(8,128)S(1)}, ...), condition=%wide.region_9.9_spmd, body=%wide.region_8.8_spmd.sunk | while | flops 135857152 | bytes 930995 | solution.py:119
  350.2 14.0 %while.126 = (s32[]{:T(128)}, f32[1,512,128]{2,1,0:T(8,128)S(1)}, s32[]{:T(128)}, s32[]{:T(128)}, bf16[1,4096,128]{2,1,0:T(8,128)(2,1)}, /*index=5*/bf16[1,512,1...) while((s32[]{:T(128)}, f32[1,512,128]{2,1,0:T(8,128)S(1)}, ...), condition=%wide.region_9.9_spmd, body=%wide.region_8.8_spmd.sunk | while | flops 135857152 | bytes 930995 | solution.py:119
  366.9 20.7 %all_to_all.83 = bf16[32,1,64,128]{3,2,1,0:T(8,128)(2,1)} all-to-all(bf16[32,1,64,128]{3,2,1,0:T(8,128)(2,1)S(1)} %get-tuple-element.820), channel_id=1, replica_groups=mesh['seq'=32,'dp'=8] {'seq'}, dimensions={0} | all-to-all | bytes 1048576 | tf_op jit(solution)/shard_map/all_to_all | solution.py:42
  387.6 5.6 all-to-all-start.7
  393.2 2.4 copy.66
  395.6 12.8 %all-to-all-done.7 = bf16[32,1,64,128]{3,2,1,0:T(8,128)(2,1)} async-done(((bf16[32,1,64,128]{3,2,1,0:T(8,128)(2,1)}), bf16[32,1,64,128]{3,2,1,0:T(8,128)(2,1)}, u32[]{:S(2)}, u32[]{:S(2)}) %all-to-all-start.7) | async-done | bytes 524320 | tf_op jit(solution)/shard_map/all_to_all | solution.py:42
  408.5 2.4 copy.67
  410.9 2.1 pad_maximum_fusion.2
  416.2 20.2 %all_to_all.84 = bf16[32,1,64,128]{3,2,1,0:T(8,128)(2,1)} all-to-all(bf16[32,1,64,128]{3,2,1,0:T(8,128)(2,1)S(1)} %get-tuple-element.818), channel_id=1, replica_groups=mesh['seq'=32,'dp'=8] {'seq'}, dimensions={0} | all-to-all | bytes 1048576 | tf_op jit(solution)/shard_map/all_to_all | solution.py:42
  436.4 5.6 all-to-all-start.9
  442.1 14.2 %all-to-all-done.9 = bf16[32,1,64,128]{3,2,1,0:T(8,128)(2,1)} async-done(((bf16[32,1,64,128]{3,2,1,0:T(8,128)(2,1)}), bf16[32,1,64,128]{3,2,1,0:T(8,128)(2,1)}, u32[]{:S(2)}, u32[]{:S(2)}) %all-to-all-start.9) | async-done | bytes 524320 | tf_op jit(solution)/shard_map/all_to_all | solution.py:42
  456.3 2.3 pad_maximum_fusion.3
  459.7 99.4 %while.124 = (s32[]{:T(128)}, bf16[1,4096,128]{2,1,0:T(8,128)(2,1)}, bf16[1,4096,128]{2,1,0:T(8,128)(2,1)}, bf16[1,4096,128]{2,1,0:T(8,128)(2,1)S(1)}, f32[1,409...) while((s32[]{:T(128)}, bf16[1,4096,128]{2,1,0:T(8,128)(2,1)}, ...), condition=%wide.region_16.17_spmd, body=%wide.region_13.16_spmd.sunk | while | flops 135922688 | bytes 1856998 | solution.py:150
  460.6 19.2 %while.127 = (s32[]{:T(128)}, f32[1,512,128]{2,1,0:T(8,128)S(1)}, s32[]{:T(128)}, bf16[1,4096,128]{2,1,0:T(8,128)(2,1)S(1)}, bf16[1,512,128]{2,1,0:T(8,128)(2,1)...) while((s32[]{:T(128)}, f32[1,512,128]{2,1,0:T(8,128)S(1)}, ...), condition=%wide.region_15.15_spmd, body=%wide.region_14.14_spmd.sunk | while | flops 135857152 | bytes 939183 | solution.py:147
  481.4 16.8 %while.127 = (s32[]{:T(128)}, f32[1,512,128]{2,1,0:T(8,128)S(1)}, s32[]{:T(128)}, bf16[1,4096,128]{2,1,0:T(8,128)(2,1)S(1)}, bf16[1,512,128]{2,1,0:T(8,128)(2,1)...) while((s32[]{:T(128)}, f32[1,512,128]{2,1,0:T(8,128)S(1)}, ...), condition=%wide.region_15.15_spmd, body=%wide.region_14.14_spmd.sunk | while | flops 135857152 | bytes 939183 | solution.py:147
  499.9 14.4 %while.127 = (s32[]{:T(128)}, f32[1,512,128]{2,1,0:T(8,128)S(1)}, s32[]{:T(128)}, bf16[1,4096,128]{2,1,0:T(8,128)(2,1)S(1)}, bf16[1,512,128]{2,1,0:T(8,128)(2,1)...) while((s32[]{:T(128)}, f32[1,512,128]{2,1,0:T(8,128)S(1)}, ...), condition=%wide.region_15.15_spmd, body=%wide.region_14.14_spmd.sunk | while | flops 135857152 | bytes 939183 | solution.py:147
  515.9 12.0 %while.127 = (s32[]{:T(128)}, f32[1,512,128]{2,1,0:T(8,128)S(1)}, s32[]{:T(128)}, bf16[1,4096,128]{2,1,0:T(8,128)(2,1)S(1)}, bf16[1,512,128]{2,1,0:T(8,128)(2,1)...) while((s32[]{:T(128)}, f32[1,512,128]{2,1,0:T(8,128)S(1)}, ...), condition=%wide.region_15.15_spmd, body=%wide.region_14.14_spmd.sunk | while | flops 135857152 | bytes 939183 | solution.py:147
  529.5 9.6 %while.127 = (s32[]{:T(128)}, f32[1,512,128]{2,1,0:T(8,128)S(1)}, s32[]{:T(128)}, bf16[1,4096,128]{2,1,0:T(8,128)(2,1)S(1)}, bf16[1,512,128]{2,1,0:T(8,128)(2,1)...) while((s32[]{:T(128)}, f32[1,512,128]{2,1,0:T(8,128)S(1)}, ...), condition=%wide.region_15.15_spmd, body=%wide.region_14.14_spmd.sunk | while | flops 135857152 | bytes 939183 | solution.py:147
  540.7 7.2 %while.127 = (s32[]{:T(128)}, f32[1,512,128]{2,1,0:T(8,128)S(1)}, s32[]{:T(128)}, bf16[1,4096,128]{2,1,0:T(8,128)(2,1)S(1)}, bf16[1,512,128]{2,1,0:T(8,128)(2,1)...) while((s32[]{:T(128)}, f32[1,512,128]{2,1,0:T(8,128)S(1)}, ...), condition=%wide.region_15.15_spmd, body=%wide.region_14.14_spmd.sunk | while | flops 135857152 | bytes 939183 | solution.py:147
  549.6 4.8 while.127
  556.0 2.4 while.127
  559.1 4.3 copy.82
  563.4 23.3 %reduce.12 = bf16[4096,128]{1,0:T(8,128)(2,1)S(1)} reduce(bf16[4096,1,128]{2,1,0:T(2,128)(2,1)} %bitcast.185, bf16[]{:T(256)} %broadcast.149), dimensions={1}, to_apply=%bitcast.143.reduce_sub_computation | reduce | bytes 2097154
  587.8 30.6 %all_to_all.87 = bf16[32,2,8192]{2,1,0:T(2,128)(2,1)S(1)} all-to-all(bf16[32,2,8192]{2,1,0:T(2,128)(2,1)} %reshape.163), channel_id=1, replica_groups=mesh['seq'=32,'dp'=8] {'seq'}, dimensions={0} | all-to-all | bytes 2097152 | tf_op jit(solution)/shard_map/all_to_all | solution.py:211
  618.5 3.5 reshape.164
  624.4 31.5 %all_to_all.85 = bf16[8,1,128,1024]{2,3,1,0:T(8,128)(2,1)S(1)} all-to-all(bf16[8,1,128,1024]{2,3,1,0:T(8,128)(2,1)S(1)} %broadcast_in_dim.44), channel_id=1, replica_groups=mesh['seq'=32,'dp'=8] {'dp'}, dimensions={0} | all-to-all | bytes 4194304 | tf_op jit(solution)/shard_map/all_to_all | solution.py:48
  657.1 33.2 %all_to_all.86 = bf16[32,32,512]{2,1,0:T(8,128)(2,1)S(1)} all-to-all(bf16[32,32,512]{2,1,0:T(8,128)(2,1)S(1)} %bitcast.203), channel_id=1, replica_groups=mesh['seq'=32,'dp'=8] {'seq'}, dimensions={0} | all-to-all | bytes 2097152 | tf_op jit(solution)/shard_map/all_to_all | solution.py:19
  (536 shorter events, 260.3 us)
Async XLA Ops:
  0.6 412.4 %copy-start = (bf16[4096,256]{1,0:T(8,128)(2,1)S(1)}, bf16[4096,256]{1,0:T(8,128)(2,1)}, u32[]{:S(2)}) copy-start(bf16[4096,256]{1,0:T(8,128)(2,1)} %param.24) | copy-start | bytes 6291460
  31.3 20.3 %all-to-all-start = ((bf16[8,2,32768]{2,1,0:T(2,128)(2,1)}), bf16[8,2,32768]{2,1,0:T(2,128)(2,1)}, u32[]{:S(2)}, u32[]{:S(2)}) async-start(bf16[8,2,32768]{2,1,0:T(2,128)(2,1)} %reshape.161), calls=%async_computation | async-start | bytes 2097152 | tf_op jit(solution)/shard_map/all_to_all | solution.py:167
  51.6 28.3 %all-to-all-start.4 = ((bf16[32,1,64,128]{3,2,1,0:T(8,128)(2,1)}), bf16[32,1,64,128]{3,2,1,0:T(8,128)(2,1)}, u32[]{:S(2)}, u32[]{:S(2)}) async-start(bf16[32,1,64,128]{3,2,1,0:T(8,128)(2,1)} %copy.59), calls=%async_computation.4 | async-start | bytes 1048576 | tf_op jit(solution)/shard_map/all_to_all | solution.py:42
  76.3 8.0 %copy-start.1 = (bf16[32,1,64,128]{2,3,0,1:T(8,128)(2,1)S(1)}, bf16[32,1,64,128]{2,3,0,1:T(8,128)(2,1)}, u32[]{:S(2)}) copy-start(bf16[32,1,64,128]{2,3,0,1:T(8,128)(2,1)} %get-tuple-element.823) | copy-start | bytes 1572868
  80.0 31.5 %all-to-all-start.1 = ((bf16[8,1,128,1024]{3,2,1,0:T(8,128)(2,1)}), bf16[8,1,128,1024]{3,2,1,0:T(8,128)(2,1)}, u32[]{:S(2)}, u32[]{:S(2)}) async-start(bf16[8,1,128,1024]{3,2,1,0:T(8,128)(2,1)} %convert_bitcast_fusion), calls=%async_computation.1 | async-start | bytes 4194304 | tf_op jit(solution)/shard_map/all_to_all | solution.py:19
  84.3 33.5 %copy-start.3 = (bf16[1,128,1024]{2,1,0:T(8,128)(2,1)S(1)}, bf16[1,128,1024]{2,1,0:T(8,128)(2,1)}, u32[]{:S(2)}) copy-start(bf16[1,128,1024]{2,1,0:T(8,128)(2,1)} %param.21) | copy-start | bytes 786436
  111.5 22.9 %all-to-all-start.5 = ((bf16[32,1,64,128]{3,2,1,0:T(8,128)(2,1)}), bf16[32,1,64,128]{3,2,1,0:T(8,128)(2,1)}, u32[]{:S(2)}, u32[]{:S(2)}) async-start(bf16[32,1,64,128]{3,2,1,0:T(8,128)(2,1)} %copy.60), calls=%async_computation.5 | async-start | bytes 1048576 | tf_op jit(solution)/shard_map/all_to_all | solution.py:42
  167.1 32.5 %all-to-all-start.3 = ((bf16[32,1,64,256]{3,2,1,0:T(8,128)(2,1)}), bf16[32,1,64,256]{3,2,1,0:T(8,128)(2,1)}, u32[]{:S(2)}, u32[]{:S(2)}) async-start(bf16[32,1,64,256]{3,2,1,0:T(8,128)(2,1)} %get-tuple-element.817), calls=%async_computation.3 | async-start | bytes 2097152 | tf_op jit(solution)/shard_map/all_to_all | solution.py:42
  387.6 20.8 %all-to-all-start.7 = ((bf16[32,1,64,128]{3,2,1,0:T(8,128)(2,1)}), bf16[32,1,64,128]{3,2,1,0:T(8,128)(2,1)}, u32[]{:S(2)}, u32[]{:S(2)}) async-start(bf16[32,1,64,128]{3,2,1,0:T(8,128)(2,1)} %get-tuple-element.821), calls=%async_computation.7 | async-start | bytes 1048576 | tf_op jit(solution)/shard_map/all_to_all | solution.py:42
  395.6 17.4 %copy-start.4 = (f32[1,128,256]{2,1,0:T(8,128)S(1)}, f32[1,128,256]{2,1,0:T(8,128)}, u32[]{:S(2)}) copy-start(f32[1,128,256]{2,1,0:T(8,128)} %param.25) | copy-start | bytes 393220
  413.0 0.8 copy-start.6
  436.4 19.8 %all-to-all-start.9 = ((bf16[32,1,64,128]{3,2,1,0:T(8,128)(2,1)}), bf16[32,1,64,128]{3,2,1,0:T(8,128)(2,1)}, u32[]{:S(2)}, u32[]{:S(2)}) async-start(bf16[32,1,64,128]{3,2,1,0:T(8,128)(2,1)} %get-tuple-element.819), calls=%async_computation.9 | async-start | bytes 1048576 | tf_op jit(solution)/shard_map/all_to_all | solution.py:42
  624.3 31.5 %copy-start.2 = (bf16[1,128,8,512]{3,1,2,0:T(8,128)(2,1)S(1)}, bf16[1,128,8,512]{3,1,2,0:T(8,128)(2,1)}, u32[]{:S(2)}) copy-start(bf16[1,128,8,512]{3,1,2,0:T(8,128)(2,1)} %copy.52) | copy-start | bytes 3145732
  657.1 33.4 %copy-start.5 = (f32[32,512]{1,0:T(8,128)S(1)}, f32[32,512]{1,0:T(8,128)}, u32[]{:S(2)}) copy-start(f32[32,512]{1,0:T(8,128)} %param.27) | copy-start | bytes 196612
where the time goes:
time: 697 us; the launch traced here: 691 us
  matrix products  172 us (25%)
  blocking collectives  169 us (24%)
  local copies, waits for them, and re-layouts  118 us (17%)
  waiting for transfers between devices  105 us (15%)
  other arithmetic  78 us (11%)
  starting transfers between devices  43.6 us (6%)
    all_to_all x3, blocking collectives, several_exchanges(): lax.all_to_all(share, axis, split_axis=0, concat_axis=0, tiled=True)  73.6 us
    all_to_all x5, waiting for transfers between devices, several_exchanges(): lax.all_to_all(share, axis, split_axis=0, concat_axis=0, tiled=True)  68.5 us
    dot_general x36, matrix products, attend_inner(): jnp.einsum('hqk,hkd->hqd', weights, v_block, preferred_element_type=jnp.f...  61.3 us
    dot_general x36, matrix products, value_inner(): jnp.einsum('hqk,hqd->hkd', weights, d_block, preferred_element_type=jnp.f...  59.8 us
    unnamed x2, other arithmetic  46.7 us
    dot_general x36, matrix products, block_scores(): jnp.einsum('hqd,hkd->hqk', q_block, k_block, preferred_element_type=jnp.f...  44.3 us
    all_to_all x5, starting transfers between devices, several_exchanges(): lax.all_to_all(share, axis, split_axis=0, concat_axis=0, tiled=True)  35 us
    unnamed x27, local copies, waits for them, and re-layouts  33.9 us
  transfers between devices with their start and end apart: 7, of which 7 were waited for; matrix products, arithmetic and copies ran while one was open for 4% of the time, Pallas kernels for 0%

commit v1 on v0

--- a/solution.py
+++ b/solution.py
@@ -164,7 +164,10 @@
     length = token_rows * seq_count
     width = min(512, length)
     scale = 1.0 / math.sqrt(HD)
-    columns = lax.all_to_all(hidden, "dp", split_axis=2, concat_axis=0, tiled=True)
+    columns = jnp.concatenate(
+        lax.all_to_all(jnp.stack(jnp.split(hidden, lax.axis_size("dp"), axis=2)), "dp", 0, 0),
+        axis=0,
+    )
     values = sum_at_owner(
         jnp.einsum("std,dk->stk", columns, value_weight, preferred_element_type=jnp.float32).astype(
             jnp.bfloat16

time: 697 us -> 678 us (0.973)
  other arithmetic: 78 us -> 54.7 us
  waiting for transfers between devices: 105 us -> 114 us
    unnamed x2 -> x1, other arithmetic: 46.7 us -> 23.4 us
    all_to_all x5, waiting for transfers between devices: 68.5 us -> 77.7 us  [several_exchanges(): lax.all_to_all(share, axis, split_axis=0, concat_axis=0, tiled=True)]
    unnamed x27 -> x30, local copies, waits for them, and re-layouts: 33.9 us -> 30.6 us
  transfers between devices with their start and end apart: 7 -> 7, of which waited for: 7 -> 7; matrix products, arithmetic and copies ran while one was open for 4% -> 3% of each run, Pallas kernels for 0% -> 0%
where the time goes in v1:
time: 678 us; the launch traced here: 672 us
  matrix products  173 us (26%)
  blocking collectives  167 us (25%)
  local copies, waits for them, and re-layouts  115 us (17%)
  waiting for transfers between devices  114 us (17%)
  other arithmetic  54.7 us (8%)
  starting transfers between devices  42.9 us (6%)
    all_to_all x5, waiting for transfers between devices, several_exchanges(): lax.all_to_all(share, axis, split_axis=0, concat_axis=0, tiled=True)  77.7 us
    all_to_all x3, blocking collectives, several_exchanges(): lax.all_to_all(share, axis, split_axis=0, concat_axis=0, tiled=True)  73.5 us
    dot_general x36, matrix products, attend_inner(): jnp.einsum('hqk,hkd->hqd', weights, v_block, preferred_element_type=jnp.f...  61.2 us
    dot_general x36, matrix products, value_inner(): jnp.einsum('hqk,hqd->hkd', weights, d_block, preferred_element_type=jnp.f...  59.8 us
    dot_general x36, matrix products, block_scores(): jnp.einsum('hqd,hkd->hqk', q_block, k_block, preferred_element_type=jnp.f...  44.3 us
    all_to_all x5, starting transfers between devices, several_exchanges(): lax.all_to_all(share, axis, split_axis=0, concat_axis=0, tiled=True)  34.3 us
    all_to_all x1, blocking collectives, sum_at_owner(): lax.all_to_all(blocks, axis, split_axis=0, concat_axis=0, tiled=True)  33.2 us
    all_to_all x1, blocking collectives, local(): lax.all_to_all(d_head, 'seq', split_axis=1, concat_axis=2, tiled=True)  30.6 us
  transfers between devices with their start and end apart: 7, of which 7 were waited for; matrix products, arithmetic and copies ran while one was open for 3% of the time, Pallas kernels for 0%

profile of v1, /device:TPU:8, one launch (start us, length us, event | category | flops | bytes accessed | tf_op | source)
XLA Modules:
  0.0 672.2 jit_solution(14405800452354773221)
XLA Ops:
  13.3 4.3 all-to-all-start
  21.0 2.5 copy.51
  23.4 10.2 %all-to-all-done = bf16[8,1,128,512]{3,2,1,0:T(8,128)(2,1)} async-done(((bf16[8,1,128,512]{3,2,1,0:T(8,128)(2,1)}), bf16[8,1,128,512]{3,2,1,0:T(8,128)(2,1)}, u32[]{:S(2)}, u32[]{:S(2)}) %all-to-all-start) | async-done | bytes 1048608 | tf_op jit(solution)/shard_map/all_to_all | solution.py:168
  33.6 11.8 %all-to-all-start.4 = ((bf16[32,1,64,128]{3,2,1,0:T(8,128)(2,1)}), bf16[32,1,64,128]{3,2,1,0:T(8,128)(2,1)}, u32[]{:S(2)}, u32[]{:S(2)}) async-start(bf16[32,1,64,128]{3,2,1,0:T(8,128)(2,1)} %copy.51), calls=%async_computation.4 | async-start | bytes 1048576 | tf_op jit(solution)/shard_map/all_to_all | solution.py:42
  45.4 3.8 convert_bitcast_fusion
  49.2 12.8 %all-to-all-done.4 = bf16[32,1,64,128]{3,2,1,0:T(8,128)(2,1)} async-done(((bf16[32,1,64,128]{3,2,1,0:T(8,128)(2,1)}), bf16[32,1,64,128]{3,2,1,0:T(8,128)(2,1)}, u32[]{:S(2)}, u32[]{:S(2)}) %all-to-all-start.4) | async-done | bytes 524320 | tf_op jit(solution)/shard_map/all_to_all | solution.py:42
  62.0 4.3 all-to-all-start.1
  67.5 26.0 %all-to-all-done.1 = bf16[8,1,128,1024]{3,2,1,0:T(8,128)(2,1)} async-done(((bf16[8,1,128,1024]{3,2,1,0:T(8,128)(2,1)}), bf16[8,1,128,1024]{3,2,1,0:T(8,128)(2,1)}, u32[]{:S(2)}, u32[]{:S(2)}) %all-to-all-start.1) | async-done | bytes 2097184 | tf_op jit(solution)/shard_map/all_to_all | solution.py:19
  93.5 5.6 all-to-all-start.5
  99.2 1.9 bitcast_reduce_fusion
  103.4 12.4 %all-to-all-done.5 = bf16[32,1,64,128]{3,2,1,0:T(8,128)(2,1)} async-done(((bf16[32,1,64,128]{3,2,1,0:T(8,128)(2,1)}), bf16[32,1,64,128]{3,2,1,0:T(8,128)(2,1)}, u32[]{:S(2)}, u32[]{:S(2)}) %all-to-all-start.5) | async-done | bytes 524320 | tf_op jit(solution)/shard_map/all_to_all | solution.py:42
  115.8 32.6 %all_to_all.69 = bf16[32,1,64,256]{3,2,1,0:T(8,128)(2,1)} all-to-all(bf16[32,1,64,256]{3,2,1,0:T(8,128)(2,1)S(1)} %get-tuple-element.816), channel_id=1, replica_groups=mesh['seq'=32,'dp'=8] {'seq'}, dimensions={0} | all-to-all | bytes 2097152 | tf_op jit(solution)/shard_map/all_to_all | solution.py:42
  148.4 5.6 all-to-all-start.3
  155.3 25.5 %all-to-all-done.3 = bf16[32,1,64,256]{3,2,1,0:T(8,128)(2,1)} async-done(((bf16[32,1,64,256]{3,2,1,0:T(8,128)(2,1)}), bf16[32,1,64,256]{3,2,1,0:T(8,128)(2,1)}, u32[]{:S(2)}, u32[]{:S(2)}) %all-to-all-start.3) | async-done | bytes 1048608 | tf_op jit(solution)/shard_map/all_to_all | solution.py:42
  180.8 3.1 pad_maximum_fusion
  183.9 4.0 reshape.164
  187.9 6.8 %fusion.74 = (bf16[4096,1,1,128]{3,1,0,2:T(2,128)(2,1)}, bf16[4096,1,1,128]{3,1,0,2:T(2,128)(2,1)}) fusion(bf16[4096,2,1,128]{3,1,0,2:T(2,128)(2,1)} %reshape.164), kind=kLoop, calls=%fused_computation.113 | loop fusion | bytes 4194304 | tf_op jit(solution)/shard_map/slice | solution.py:198
  194.7 5.4 copy.66
  200.1 2.3 copy.61
  203.6 59.3 %while.120 = (s32[]{:T(128)}, f32[1,4096]{1,0:T(1,128)}, f32[1,4096]{1,0:T(1,128)}, bf16[1,4096,128]{2,1,0:T(8,128)(2,1)S(1)}, bf16[1,4096,128]{2,1,0:T(8,128)(2...) while((s32[]{:T(128)}, f32[1,4096]{1,0:T(1,128)}, ...), condition=%wide.region_6.7_spmd, body=%wide.region_1.6_spmd.sunk | while | flops 68683792 | bytes 2669010 | solution.py:94
  205.8 3.0 while.125
  209.5 4.5 while.125
  214.6 6.0 while.125
  221.3 7.5 %while.125 = (s32[]{:T(128)}, f32[1,512]{1,0:T(1,128)S(1)}, f32[1,512]{1,0:T(1,128)S(1)}, s32[]{:T(128)}, s32[]{:T(128)}, /*index=5*/bf16[1,4096,128]{2,1,0:T(8,...) while((s32[]{:T(128)}, f32[1,512]{1,0:T(1,128)S(1)}, ...), condition=%wide.region_5.5_spmd, body=%wide.region_2.4_spmd.sunk | while | flops 68683784 | bytes 2394279 | solution.py:88
  229.5 9.0 %while.125 = (s32[]{:T(128)}, f32[1,512]{1,0:T(1,128)S(1)}, f32[1,512]{1,0:T(1,128)S(1)}, s32[]{:T(128)}, s32[]{:T(128)}, /*index=5*/bf16[1,4096,128]{2,1,0:T(8,...) while((s32[]{:T(128)}, f32[1,512]{1,0:T(1,128)S(1)}, ...), condition=%wide.region_5.5_spmd, body=%wide.region_2.4_spmd.sunk | while | flops 68683784 | bytes 2394279 | solution.py:88
  239.1 10.5 %while.125 = (s32[]{:T(128)}, f32[1,512]{1,0:T(1,128)S(1)}, f32[1,512]{1,0:T(1,128)S(1)}, s32[]{:T(128)}, s32[]{:T(128)}, /*index=5*/bf16[1,4096,128]{2,1,0:T(8,...) while((s32[]{:T(128)}, f32[1,512]{1,0:T(1,128)S(1)}, ...), condition=%wide.region_5.5_spmd, body=%wide.region_2.4_spmd.sunk | while | flops 68683784 | bytes 2394279 | solution.py:88
  250.3 12.1 %while.125 = (s32[]{:T(128)}, f32[1,512]{1,0:T(1,128)S(1)}, f32[1,512]{1,0:T(1,128)S(1)}, s32[]{:T(128)}, s32[]{:T(128)}, /*index=5*/bf16[1,4096,128]{2,1,0:T(8,...) while((s32[]{:T(128)}, f32[1,512]{1,0:T(1,128)S(1)}, ...), condition=%wide.region_5.5_spmd, body=%wide.region_2.4_spmd.sunk | while | flops 68683784 | bytes 2394279 | solution.py:88
  263.0 5.4 copy.67
  268.4 2.3 copy.55
  271.8 74.2 %while.122 = (s32[]{:T(128)}, bf16[1,4096,128]{2,1,0:T(8,128)(2,1)}, bf16[1,4096,128]{2,1,0:T(8,128)(2,1)S(1)}, f32[1,4096]{1,0:T(1,128)}, f32[1,4096]{1,0:T(1,1...) while((s32[]{:T(128)}, bf16[1,4096,128]{2,1,0:T(8,128)(2,1)}, ...), condition=%wide.region_10.11_spmd, body=%wide.region_7.10_spmd.sunk | while | flops 135922688 | bytes 1857014 | solution.py:122
  275.7 3.5 while.126
  280.6 5.2 while.126
  287.3 7.0 %while.126 = (s32[]{:T(128)}, f32[1,512,128]{2,1,0:T(8,128)S(1)}, s32[]{:T(128)}, s32[]{:T(128)}, bf16[1,4096,128]{2,1,0:T(8,128)(2,1)}, /*index=5*/bf16[1,512,1...) while((s32[]{:T(128)}, f32[1,512,128]{2,1,0:T(8,128)S(1)}, ...), condition=%wide.region_9.9_spmd, body=%wide.region_8.8_spmd.sunk | while | flops 135857152 | bytes 930995 | solution.py:119
  295.7 8.7 %while.126 = (s32[]{:T(128)}, f32[1,512,128]{2,1,0:T(8,128)S(1)}, s32[]{:T(128)}, s32[]{:T(128)}, bf16[1,4096,128]{2,1,0:T(8,128)(2,1)}, /*index=5*/bf16[1,512,1...) while((s32[]{:T(128)}, f32[1,512,128]{2,1,0:T(8,128)S(1)}, ...), condition=%wide.region_9.9_spmd, body=%wide.region_8.8_spmd.sunk | while | flops 135857152 | bytes 930995 | solution.py:119
  305.8 10.5 %while.126 = (s32[]{:T(128)}, f32[1,512,128]{2,1,0:T(8,128)S(1)}, s32[]{:T(128)}, s32[]{:T(128)}, bf16[1,4096,128]{2,1,0:T(8,128)(2,1)}, /*index=5*/bf16[1,512,1...) while((s32[]{:T(128)}, f32[1,512,128]{2,1,0:T(8,128)S(1)}, ...), condition=%wide.region_9.9_spmd, body=%wide.region_8.8_spmd.sunk | while | flops 135857152 | bytes 930995 | solution.py:119
  317.7 12.2 %while.126 = (s32[]{:T(128)}, f32[1,512,128]{2,1,0:T(8,128)S(1)}, s32[]{:T(128)}, s32[]{:T(128)}, bf16[1,4096,128]{2,1,0:T(8,128)(2,1)}, /*index=5*/bf16[1,512,1...) while((s32[]{:T(128)}, f32[1,512,128]{2,1,0:T(8,128)S(1)}, ...), condition=%wide.region_9.9_spmd, body=%wide.region_8.8_spmd.sunk | while | flops 135857152 | bytes 930995 | solution.py:119
  331.3 14.0 %while.126 = (s32[]{:T(128)}, f32[1,512,128]{2,1,0:T(8,128)S(1)}, s32[]{:T(128)}, s32[]{:T(128)}, bf16[1,4096,128]{2,1,0:T(8,128)(2,1)}, /*index=5*/bf16[1,512,1...) while((s32[]{:T(128)}, f32[1,512,128]{2,1,0:T(8,128)S(1)}, ...), condition=%wide.region_9.9_spmd, body=%wide.region_8.8_spmd.sunk | while | flops 135857152 | bytes 930995 | solution.py:119
  346.0 2.1 slice_bitcast_fusion.1
  348.0 20.7 %all_to_all.70 = bf16[32,1,64,128]{3,2,1,0:T(8,128)(2,1)} all-to-all(bf16[32,1,64,128]{3,2,1,0:T(8,128)(2,1)S(1)} %get-tuple-element.820), channel_id=1, replica_groups=mesh['seq'=32,'dp'=8] {'seq'}, dimensions={0} | all-to-all | bytes 1048576 | tf_op jit(solution)/shard_map/all_to_all | solution.py:42
  368.7 5.6 all-to-all-start.7
  374.4 2.4 copy.58
  376.8 12.8 %all-to-all-done.7 = bf16[32,1,64,128]{3,2,1,0:T(8,128)(2,1)} async-done(((bf16[32,1,64,128]{3,2,1,0:T(8,128)(2,1)}), bf16[32,1,64,128]{3,2,1,0:T(8,128)(2,1)}, u32[]{:S(2)}, u32[]{:S(2)}) %all-to-all-start.7) | async-done | bytes 524320 | tf_op jit(solution)/shard_map/all_to_all | solution.py:42
  389.6 2.4 copy.59
  392.0 2.1 pad_maximum_fusion.2
  397.3 20.2 %all_to_all.71 = bf16[32,1,64,128]{3,2,1,0:T(8,128)(2,1)} all-to-all(bf16[32,1,64,128]{3,2,1,0:T(8,128)(2,1)S(1)} %get-tuple-element.818), channel_id=1, replica_groups=mesh['seq'=32,'dp'=8] {'seq'}, dimensions={0} | all-to-all | bytes 1048576 | tf_op jit(solution)/shard_map/all_to_all | solution.py:42
  417.5 5.6 all-to-all-start.9
  423.2 14.2 %all-to-all-done.9 = bf16[32,1,64,128]{3,2,1,0:T(8,128)(2,1)} async-done(((bf16[32,1,64,128]{3,2,1,0:T(8,128)(2,1)}), bf16[32,1,64,128]{3,2,1,0:T(8,128)(2,1)}, u32[]{:S(2)}, u32[]{:S(2)}) %all-to-all-start.9) | async-done | bytes 524320 | tf_op jit(solution)/shard_map/all_to_all | solution.py:42
  437.4 2.3 pad_maximum_fusion.3
  440.8 99.4 %while.124 = (s32[]{:T(128)}, bf16[1,4096,128]{2,1,0:T(8,128)(2,1)}, bf16[1,4096,128]{2,1,0:T(8,128)(2,1)}, bf16[1,4096,128]{2,1,0:T(8,128)(2,1)S(1)}, f32[1,409...) while((s32[]{:T(128)}, bf16[1,4096,128]{2,1,0:T(8,128)(2,1)}, ...), condition=%wide.region_16.17_spmd, body=%wide.region_13.16_spmd.sunk | while | flops 135922688 | bytes 1856998 | solution.py:150
  441.7 19.2 %while.127 = (s32[]{:T(128)}, f32[1,512,128]{2,1,0:T(8,128)S(1)}, s32[]{:T(128)}, bf16[1,4096,128]{2,1,0:T(8,128)(2,1)S(1)}, bf16[1,512,128]{2,1,0:T(8,128)(2,1)...) while((s32[]{:T(128)}, f32[1,512,128]{2,1,0:T(8,128)S(1)}, ...), condition=%wide.region_15.15_spmd, body=%wide.region_14.14_spmd.sunk | while | flops 135857152 | bytes 939183 | solution.py:147
  462.6 16.8 %while.127 = (s32[]{:T(128)}, f32[1,512,128]{2,1,0:T(8,128)S(1)}, s32[]{:T(128)}, bf16[1,4096,128]{2,1,0:T(8,128)(2,1)S(1)}, bf16[1,512,128]{2,1,0:T(8,128)(2,1)...) while((s32[]{:T(128)}, f32[1,512,128]{2,1,0:T(8,128)S(1)}, ...), condition=%wide.region_15.15_spmd, body=%wide.region_14.14_spmd.sunk | while | flops 135857152 | bytes 939183 | solution.py:147
  481.0 14.4 %while.127 = (s32[]{:T(128)}, f32[1,512,128]{2,1,0:T(8,128)S(1)}, s32[]{:T(128)}, bf16[1,4096,128]{2,1,0:T(8,128)(2,1)S(1)}, bf16[1,512,128]{2,1,0:T(8,128)(2,1)...) while((s32[]{:T(128)}, f32[1,512,128]{2,1,0:T(8,128)S(1)}, ...), condition=%wide.region_15.15_spmd, body=%wide.region_14.14_spmd.sunk | while | flops 135857152 | bytes 939183 | solution.py:147
  497.0 12.0 %while.127 = (s32[]{:T(128)}, f32[1,512,128]{2,1,0:T(8,128)S(1)}, s32[]{:T(128)}, bf16[1,4096,128]{2,1,0:T(8,128)(2,1)S(1)}, bf16[1,512,128]{2,1,0:T(8,128)(2,1)...) while((s32[]{:T(128)}, f32[1,512,128]{2,1,0:T(8,128)S(1)}, ...), condition=%wide.region_15.15_spmd, body=%wide.region_14.14_spmd.sunk | while | flops 135857152 | bytes 939183 | solution.py:147
  510.6 9.6 %while.127 = (s32[]{:T(128)}, f32[1,512,128]{2,1,0:T(8,128)S(1)}, s32[]{:T(128)}, bf16[1,4096,128]{2,1,0:T(8,128)(2,1)S(1)}, bf16[1,512,128]{2,1,0:T(8,128)(2,1)...) while((s32[]{:T(128)}, f32[1,512,128]{2,1,0:T(8,128)S(1)}, ...), condition=%wide.region_15.15_spmd, body=%wide.region_14.14_spmd.sunk | while | flops 135857152 | bytes 939183 | solution.py:147
  521.9 7.2 %while.127 = (s32[]{:T(128)}, f32[1,512,128]{2,1,0:T(8,128)S(1)}, s32[]{:T(128)}, bf16[1,4096,128]{2,1,0:T(8,128)(2,1)S(1)}, bf16[1,512,128]{2,1,0:T(8,128)(2,1)...) while((s32[]{:T(128)}, f32[1,512,128]{2,1,0:T(8,128)S(1)}, ...), condition=%wide.region_15.15_spmd, body=%wide.region_14.14_spmd.sunk | while | flops 135857152 | bytes 939183 | solution.py:147
  530.7 4.8 while.127
  537.1 2.4 while.127
  540.2 4.3 copy.73
  545.0 23.4 %reduce.11 = bf16[4096,128]{1,0:T(8,128)(2,1)S(1)} reduce(bf16[4096,1,128]{2,1,0:T(2,128)(2,1)} %bitcast.194, bf16[]{:T(256)} %broadcast.149), dimensions={1}, to_apply=%bitcast.154.reduce_sub_computation | reduce | bytes 2097154
  569.6 30.6 %all_to_all.74 = bf16[32,2,8192]{2,1,0:T(2,128)(2,1)S(1)} all-to-all(bf16[32,2,8192]{2,1,0:T(2,128)(2,1)} %reshape.165), channel_id=1, replica_groups=mesh['seq'=32,'dp'=8] {'seq'}, dimensions={0} | all-to-all | bytes 2097152 | tf_op jit(solution)/shard_map/all_to_all | solution.py:214
  600.2 3.5 reshape.166
  606.1 29.7 %all_to_all.72 = bf16[8,1,128,1024]{2,3,1,0:T(8,128)(2,1)S(1)} all-to-all(bf16[8,1,128,1024]{2,3,1,0:T(8,128)(2,1)S(1)} %broadcast_in_dim.44), channel_id=1, replica_groups=mesh['seq'=32,'dp'=8] {'dp'}, dimensions={0} | all-to-all | bytes 4194304 | tf_op jit(solution)/shard_map/all_to_all | solution.py:48
  635.7 2.5 bitcast_convert_fusion
  638.2 33.2 %all_to_all.73 = bf16[32,32,512]{2,1,0:T(8,128)(2,1)S(1)} all-to-all(bf16[32,32,512]{2,1,0:T(8,128)(2,1)S(1)} %bitcast.211), channel_id=1, replica_groups=mesh['seq'=32,'dp'=8] {'seq'}, dimensions={0} | all-to-all | bytes 2097152 | tf_op jit(solution)/shard_map/all_to_all | solution.py:19
  (538 shorter events, 263.4 us)
Async XLA Ops:
  0.6 393.5 %copy-start = (bf16[4096,256]{1,0:T(8,128)(2,1)S(1)}, bf16[4096,256]{1,0:T(8,128)(2,1)}, u32[]{:S(2)}) copy-start(bf16[4096,256]{1,0:T(8,128)(2,1)} %param.24) | copy-start | bytes 6291460
  13.3 20.3 %all-to-all-start = ((bf16[8,1,128,512]{3,2,1,0:T(8,128)(2,1)}), bf16[8,1,128,512]{3,2,1,0:T(8,128)(2,1)}, u32[]{:S(2)}, u32[]{:S(2)}) async-start(bf16[8,1,128,512]{3,2,1,0:T(8,128)(2,1)} %bitcast_dynamic-update-slice_fusion), calls=%async_computation | async-start | bytes 2097152 | tf_op jit(solution)/shard_map/all_to_all | solution.py:168
  21.0 24.4 %copy-start.6 = (bf16[512,1024]{1,0:T(8,128)(2,1)S(1)}, bf16[512,1024]{1,0:T(8,128)(2,1)}, u32[]{:S(2)}) copy-start(bf16[512,1024]{1,0:T(8,128)(2,1)} %param.23) | copy-start | bytes 3145732
  33.6 28.3 %all-to-all-start.4 = ((bf16[32,1,64,128]{3,2,1,0:T(8,128)(2,1)}), bf16[32,1,64,128]{3,2,1,0:T(8,128)(2,1)}, u32[]{:S(2)}, u32[]{:S(2)}) async-start(bf16[32,1,64,128]{3,2,1,0:T(8,128)(2,1)} %copy.51), calls=%async_computation.4 | async-start | bytes 1048576 | tf_op jit(solution)/shard_map/all_to_all | solution.py:42
  49.2 17.1 %copy-start.1 = (bf16[32,1,64,128]{2,3,0,1:T(8,128)(2,1)S(1)}, bf16[32,1,64,128]{2,3,0,1:T(8,128)(2,1)}, u32[]{:S(2)}) copy-start(bf16[32,1,64,128]{2,3,0,1:T(8,128)(2,1)} %get-tuple-element.823) | copy-start | bytes 1572868
  62.0 31.5 %all-to-all-start.1 = ((bf16[8,1,128,1024]{3,2,1,0:T(8,128)(2,1)}), bf16[8,1,128,1024]{3,2,1,0:T(8,128)(2,1)}, u32[]{:S(2)}, u32[]{:S(2)}) async-start(bf16[8,1,128,1024]{3,2,1,0:T(8,128)(2,1)} %convert_bitcast_fusion), calls=%async_computation.1 | async-start | bytes 4194304 | tf_op jit(solution)/shard_map/all_to_all | solution.py:19
  66.3 32.8 %copy-start.2 = (bf16[1,128,1024]{2,1,0:T(8,128)(2,1)S(1)}, bf16[1,128,1024]{2,1,0:T(8,128)(2,1)}, u32[]{:S(2)}) copy-start(bf16[1,128,1024]{2,1,0:T(8,128)(2,1)} %param.21) | copy-start | bytes 786436
  93.5 22.3 %all-to-all-start.5 = ((bf16[32,1,64,128]{3,2,1,0:T(8,128)(2,1)}), bf16[32,1,64,128]{3,2,1,0:T(8,128)(2,1)}, u32[]{:S(2)}, u32[]{:S(2)}) async-start(bf16[32,1,64,128]{3,2,1,0:T(8,128)(2,1)} %copy.52), calls=%async_computation.5 | async-start | bytes 1048576 | tf_op jit(solution)/shard_map/all_to_all | solution.py:42
  148.4 32.4 %all-to-all-start.3 = ((bf16[32,1,64,256]{3,2,1,0:T(8,128)(2,1)}), bf16[32,1,64,256]{3,2,1,0:T(8,128)(2,1)}, u32[]{:S(2)}, u32[]{:S(2)}) async-start(bf16[32,1,64,256]{3,2,1,0:T(8,128)(2,1)} %get-tuple-element.817), calls=%async_computation.3 | async-start | bytes 2097152 | tf_op jit(solution)/shard_map/all_to_all | solution.py:42
  368.7 20.8 %all-to-all-start.7 = ((bf16[32,1,64,128]{3,2,1,0:T(8,128)(2,1)}), bf16[32,1,64,128]{3,2,1,0:T(8,128)(2,1)}, u32[]{:S(2)}, u32[]{:S(2)}) async-start(bf16[32,1,64,128]{3,2,1,0:T(8,128)(2,1)} %get-tuple-element.821), calls=%async_computation.7 | async-start | bytes 1048576 | tf_op jit(solution)/shard_map/all_to_all | solution.py:42
  376.8 17.4 %copy-start.3 = (f32[1,128,256]{2,1,0:T(8,128)S(1)}, f32[1,128,256]{2,1,0:T(8,128)}, u32[]{:S(2)}) copy-start(f32[1,128,256]{2,1,0:T(8,128)} %param.25) | copy-start | bytes 393220
  394.1 0.8 copy-start.5
  417.5 19.8 %all-to-all-start.9 = ((bf16[32,1,64,128]{3,2,1,0:T(8,128)(2,1)}), bf16[32,1,64,128]{3,2,1,0:T(8,128)(2,1)}, u32[]{:S(2)}, u32[]{:S(2)}) async-start(bf16[32,1,64,128]{3,2,1,0:T(8,128)(2,1)} %get-tuple-element.819), calls=%async_computation.9 | async-start | bytes 1048576 | tf_op jit(solution)/shard_map/all_to_all | solution.py:42
  638.2 33.4 %copy-start.4 = (f32[32,512]{1,0:T(8,128)S(1)}, f32[32,512]{1,0:T(8,128)}, u32[]{:S(2)}) copy-start(f32[32,512]{1,0:T(8,128)} %param.27) | copy-start | bytes 196612
